TPU v7x, 256 devices: a whole 4x4x8 slice. The times are simulated.
256 devices in a mesh: sweep: 16 (over x_lo, y, core), span: 16 (over x_hi, z).
Axes of the slice: x: 4 (x_hi: 2, x_lo: 2; x = x_hi * 2 + x_lo), y: 4, z: 8, core: 2. Of those that a mesh axis runs over, the one named last changes fastest.
Arguments:
- right_side: float32 [32, 16, 625, 512], P('sweep', 'span'), may hold values from -6 to 6
- start_field: float32 [32, 16, 625, 512], P('sweep', 'span'), may hold values from -6 to 6
- block_inverse: float32 [32, 16, 625, 625], P('sweep', 'span'), may hold values from -0.25 to 0.25
- upwind_block: float32 [32, 16, 625, 125], P('sweep', 'span'), may hold values from -1 to 1
- south_block: float32 [32, 16, 625, 125], P('sweep', 'span'), may hold values from -0.625 to 0.625
- north_block: float32 [32, 16, 625, 125], P('sweep', 'span'), may hold values from -0.625 to 0.625
Outputs:
- solution: float32 [32, 16, 625, 512], P('sweep', 'span')
All inputs are finite; a program needn't handle non-finite values.
Results may differ from a plain program's by a relative error of at most 0.00022.
Values sent between devices are 32-bit elements; how exact they have to be, the bound alone decides.
A program may use at most 128 MiB of HBM per device.

v0:
```python
import jax
import jax.numpy as jnp
from jax import lax
from jax.sharding import PartitionSpec as P

VARS = 5
NODE = 5
FACE = 125
FRONTS = 4
SWEEPS = 2


def passed_along(shard, axis, by):
    count = lax.axis_size(axis)
    pairs = [(i, i + by) for i in range(count) if 0 <= i + by < count]
    return lax.ppermute(shard, axis, pairs)


def from_behind(shard, axis, by):
    count = lax.axis_size(axis)
    return lax.ppermute(shard, axis, [(i, (i + by) % count) for i in range(count)])


def face_grid(field):
    leading = field.shape[:-2]
    return field.reshape(leading + (VARS, NODE, NODE, NODE, field.shape[-1]))


def down_face(field):
    leading = field.shape[:-2]
    return face_grid(field)[..., :, NODE - 1, :, :, :].reshape(leading + (FACE, field.shape[-1]))


def high_face(field):
    leading = field.shape[:-2]
    return face_grid(field)[..., :, :, NODE - 1, :, :].reshape(leading + (FACE, field.shape[-1]))


def low_face(field):
    leading = field.shape[:-2]
    return face_grid(field)[..., :, :, 0, :, :].reshape(leading + (FACE, field.shape[-1]))


def product(matrix, vectors):
    return jnp.dot(
        matrix, vectors, precision=lax.Precision.HIGHEST, preferred_element_type=jnp.float32
    )


def batched_product(matrix, vectors):
    return jnp.einsum("eab,ebr->ear", matrix, vectors, precision=lax.Precision.HIGHEST)


def slab_solve(inverse_local, upwind_local, inflow, forcing):
    pieces = []
    for element in range(forcing.shape[0]):
        residual = forcing[element] - product(upwind_local[element], inflow)
        solved = product(inverse_local[element], residual)
        pieces.append(solved)
        inflow = down_face(solved)
    return (jnp.stack(pieces), inflow)


def front_chain(inverse_local, upwind_local, forcing, sections, device_pos):
    columns = forcing.shape[-1]
    panel_width = columns // FRONTS

    def section_step(step_no, state_pair):
        field_new, outgoing = state_pair
        incoming = passed_along(outgoing, "sweep", 1)
        front_no = step_no - device_pos
        active = jnp.logical_and(front_no >= 0, front_no < FRONTS)
        chosen = jnp.clip(front_no, 0, FRONTS - 1) * panel_width

        def advance(current):
            panel_rhs = lax.dynamic_slice_in_dim(forcing, chosen, panel_width, 2)
            solved, leaving = slab_solve(inverse_local, upwind_local, incoming, panel_rhs)
            return (lax.dynamic_update_slice_in_dim(current, solved, chosen, 2), leaving)

        def remain(current):
            return (current, jnp.zeros_like(incoming))

        return lax.cond(active, advance, remain, field_new)

    initial = (jnp.zeros_like(forcing), jnp.zeros((FACE, panel_width), jnp.float32))
    field_new, _ = lax.fori_loop(0, sections + FRONTS - 1, section_step, initial)
    return field_new


def per_device(right_side, start_field, block_inverse, upwind_block, south_block, north_block):
    rhs_local = right_side[:, 0]
    field = start_field[:, 0]
    inverse_local = block_inverse[:, 0]
    upwind_local = upwind_block[:, 0]
    south_local = south_block[:, 0]
    north_local = north_block[:, 0]
    sections = lax.axis_size("sweep")
    device_pos = lax.axis_index("sweep")
    for sweep_no in range(SWEEPS):
        south_traces = from_behind(high_face(field), "span", 1)
        north_traces = from_behind(low_face(field), "span", -1)
        forcing = (
            rhs_local
            - batched_product(south_local, south_traces)
            - batched_product(north_local, north_traces)
        )
        field = front_chain(inverse_local, upwind_local, forcing, sections, device_pos)
    return field[:, None]


def solution(mesh):
    return jax.shard_map(
        per_device,
        mesh=mesh,
        in_specs=(
            P("sweep", "span", None, None),
            P("sweep", "span", None, None),
            P("sweep", "span", None, None),
            P("sweep", "span", None, None),
            P("sweep", "span", None, None),
            P("sweep", "span", None, None),
        ),
        out_specs=P("sweep", "span", None, None),
        check_vma=False,
    )
```

profile of v0, /device:TPU:27, one launch (start us, length us, event | category | flops | bytes accessed | tf_op | source)
XLA Modules:
  0.0 728.6 jit_solution(12167683109356460010)
XLA Ops:
  6.8 5.5 collective-permute-start.3
  14.3 9.1 %collective-permute-done.2 = f32[2,125,512]{2,1,0:T(8,128)} collective-permute-done((f32[2,125,512]{2,1,0:T(8,128)}, f32[2,125,512]{2,1,0:T(8,128)}, u32[]{:S(2)}, u32[]{:S(2)}) %collective-permute-start.2) | collective-permute-done | bytes 512032 | tf_op jit(solution)/shard_map/ppermute | solution.py:21
  34.3 377.7 %while.36 = (s32[]{:T(128)}, f32[2,625,512]{2,1,0:T(8,128)}, f32[125,128]{1,0:T(8,128)}, s32[]{:T(128)}, f32[2,625,512]{2,1,0:T(8,128)}, /*index=5*/f32[2,625,12...) while((s32[]{:T(128)}, f32[2,625,512]{2,1,0:T(8,128)}, f32[125,128]{1,0:T(8,128)}, ...), condition=%wide.region_3.4_spmd, body=%wide.region_0.3_spmd.sunk | while | flops 1440320000 | bytes 12480909 | solution.py:86
  117.9 6.6 collective-permute-done
  126.4 6.6 collective-permute-done
  134.9 192.2 %collective-permute-done = f32[125,128]{1,0:T(8,128)S(1)} collective-permute-done((f32[125,128]{1,0:T(8,128)}, f32[125,128]{1,0:T(8,128)S(1)}, u32[]{:S(2)}, u32[]{:S(2)}) %collective-permute-start) | collective-permute-done | bytes 64032 | tf_op jit(solution)/shard_map/while/body/eval_jaxpr/ppermute | solution.py:16
  327.1 15.4 %conditional.4 = (f32[2,625,512]{2,1,0:T(8,128)}, f32[125,128]{1,0:T(8,128)}) conditional(s32[]{:T(128)} %convert_element_type.16, f32[2,625,512]{2,1,0:T(8,128)} %get-tuple-element.490, (s32[]{:T(128)}, f32[2,625,512]{2,1,0:T(8,128)}, f32[2,625,125]{2,1,0:T(8,128)}, f32[125,128]{1,0:T(8,128)S(1)}, f32[2,625,625]{2,1,0:T(8,128)S(1)}, ...), branch_computations={%region_1.1_spmd, %region_2.2_spmd} | conditional | flops 1440320000 | bytes 12224682 | solution.py:83
  343.8 6.3 collective-permute-done
  350.1 15.3 %conditional.4 = (f32[2,625,512]{2,1,0:T(8,128)}, f32[125,128]{1,0:T(8,128)}) conditional(s32[]{:T(128)} %convert_element_type.16, f32[2,625,512]{2,1,0:T(8,128)} %get-tuple-element.490, (s32[]{:T(128)}, f32[2,625,512]{2,1,0:T(8,128)}, f32[2,625,125]{2,1,0:T(8,128)}, f32[125,128]{1,0:T(8,128)S(1)}, f32[2,625,625]{2,1,0:T(8,128)S(1)}, ...), branch_computations={%region_1.1_spmd, %region_2.2_spmd} | conditional | flops 1440320000 | bytes 12224682 | solution.py:83
  366.7 6.8 collective-permute-done
  373.5 15.4 %conditional.4 = (f32[2,625,512]{2,1,0:T(8,128)}, f32[125,128]{1,0:T(8,128)}) conditional(s32[]{:T(128)} %convert_element_type.16, f32[2,625,512]{2,1,0:T(8,128)} %get-tuple-element.490, (s32[]{:T(128)}, f32[2,625,512]{2,1,0:T(8,128)}, f32[2,625,125]{2,1,0:T(8,128)}, f32[125,128]{1,0:T(8,128)S(1)}, f32[2,625,625]{2,1,0:T(8,128)S(1)}, ...), branch_computations={%region_1.1_spmd, %region_2.2_spmd} | conditional | flops 1440320000 | bytes 12224682 | solution.py:83
  390.2 6.6 collective-permute-done
  396.7 15.4 %conditional.4 = (f32[2,625,512]{2,1,0:T(8,128)}, f32[125,128]{1,0:T(8,128)}) conditional(s32[]{:T(128)} %convert_element_type.16, f32[2,625,512]{2,1,0:T(8,128)} %get-tuple-element.490, (s32[]{:T(128)}, f32[2,625,512]{2,1,0:T(8,128)}, f32[2,625,125]{2,1,0:T(8,128)}, f32[125,128]{1,0:T(8,128)S(1)}, f32[2,625,625]{2,1,0:T(8,128)S(1)}, ...), branch_computations={%region_1.1_spmd, %region_2.2_spmd} | conditional | flops 1440320000 | bytes 12224682 | solution.py:83
  423.0 6.0 collective-permute-done.4
  440.0 282.8 %while.37 = (s32[]{:T(128)}, f32[2,625,512]{2,1,0:T(8,128)}, f32[125,128]{1,0:T(8,128)}, s32[]{:T(128)}, f32[2,625,512]{2,1,0:T(8,128)}, /*index=5*/f32[2,625,12...) while((s32[]{:T(128)}, f32[2,625,512]{2,1,0:T(8,128)}, f32[125,128]{1,0:T(8,128)}, ...), condition=%wide.region_7.8_spmd, body=%wide.region_4.7_spmd.sunk | while | flops 1440320000 | bytes 12480909 | solution.py:86
  532.2 105.6 %collective-permute-done.1 = f32[125,128]{1,0:T(8,128)S(1)} collective-permute-done((f32[125,128]{1,0:T(8,128)}, f32[125,128]{1,0:T(8,128)S(1)}, u32[]{:S(2)}, u32[]{:S(2)}) %collective-permute-start.1) | collective-permute-done | bytes 64032 | tf_op jit(solution)/shard_map/while/body/eval_jaxpr/ppermute | solution.py:16
  637.8 15.4 %conditional.5 = (f32[2,625,512]{2,1,0:T(8,128)}, f32[125,128]{1,0:T(8,128)}) conditional(s32[]{:T(128)} %convert_element_type.17, f32[2,625,512]{2,1,0:T(8,128)} %get-tuple-element.520, (s32[]{:T(128)}, f32[2,625,512]{2,1,0:T(8,128)}, f32[2,625,125]{2,1,0:T(8,128)}, f32[125,128]{1,0:T(8,128)S(1)}, f32[2,625,625]{2,1,0:T(8,128)S(1)}, ...), branch_computations={%region_5.5_spmd, %region_6.6_spmd} | conditional | flops 1440320000 | bytes 12224682 | solution.py:83
  654.5 6.3 collective-permute-done.1
  660.8 15.3 %conditional.5 = (f32[2,625,512]{2,1,0:T(8,128)}, f32[125,128]{1,0:T(8,128)}) conditional(s32[]{:T(128)} %convert_element_type.17, f32[2,625,512]{2,1,0:T(8,128)} %get-tuple-element.520, (s32[]{:T(128)}, f32[2,625,512]{2,1,0:T(8,128)}, f32[2,625,125]{2,1,0:T(8,128)}, f32[125,128]{1,0:T(8,128)S(1)}, f32[2,625,625]{2,1,0:T(8,128)S(1)}, ...), branch_computations={%region_5.5_spmd, %region_6.6_spmd} | conditional | flops 1440320000 | bytes 12224682 | solution.py:83
  677.4 6.8 collective-permute-done.1
  684.2 15.4 %conditional.5 = (f32[2,625,512]{2,1,0:T(8,128)}, f32[125,128]{1,0:T(8,128)}) conditional(s32[]{:T(128)} %convert_element_type.17, f32[2,625,512]{2,1,0:T(8,128)} %get-tuple-element.520, (s32[]{:T(128)}, f32[2,625,512]{2,1,0:T(8,128)}, f32[2,625,125]{2,1,0:T(8,128)}, f32[125,128]{1,0:T(8,128)S(1)}, f32[2,625,625]{2,1,0:T(8,128)S(1)}, ...), branch_computations={%region_5.5_spmd, %region_6.6_spmd} | conditional | flops 1440320000 | bytes 12224682 | solution.py:83
  700.9 6.6 collective-permute-done.1
  707.5 15.4 %conditional.5 = (f32[2,625,512]{2,1,0:T(8,128)}, f32[125,128]{1,0:T(8,128)}) conditional(s32[]{:T(128)} %convert_element_type.17, f32[2,625,512]{2,1,0:T(8,128)} %get-tuple-element.520, (s32[]{:T(128)}, f32[2,625,512]{2,1,0:T(8,128)}, f32[2,625,125]{2,1,0:T(8,128)}, f32[125,128]{1,0:T(8,128)S(1)}, f32[2,625,625]{2,1,0:T(8,128)S(1)}, ...), branch_computations={%region_5.5_spmd, %region_6.6_spmd} | conditional | flops 1440320000 | bytes 12224682 | solution.py:83
  722.8 5.8 copy.21
  (281 shorter events, 369.4 us)
Async XLA Ops:
  4.3 19.1 %collective-permute-start.2 = (f32[2,125,512]{2,1,0:T(8,128)}, f32[2,125,512]{2,1,0:T(8,128)}, u32[]{:S(2)}, u32[]{:S(2)}) collective-permute-start(f32[2,125,512]{2,1,0:T(8,128)} %copy.16), channel_id=1, source_target_pairs={{0,1},{1,2},{2,3},{3,4},{4,5},{5,6},{6,7},{7,8},{8,9},{9,10},{10,1... | collective-permute-start | bytes 1536008 | tf_op jit(solution)/shard_map/ppermute | solution.py:21
  6.8 20.0 %collective-permute-start.3 = (f32[2,125,512]{2,1,0:T(8,128)}, f32[2,125,512]{2,1,0:T(8,128)}, u32[]{:S(2)}, u32[]{:S(2)}) collective-permute-start(f32[2,125,512]{2,1,0:T(8,128)} %copy.17), channel_id=1, source_target_pairs={{0,15},{1,0},{2,1},{3,2},{4,3},{5,4},{6,5},{7,6},{8,7},{9,8},{10,9... | collective-permute-start | bytes 1536008 | tf_op jit(solution)/shard_map/ppermute | solution.py:21
  51.9 5.8 collective-permute-start
  58.3 5.8 collective-permute-start
  64.7 5.8 collective-permute-start
  71.1 5.8 collective-permute-start
  77.5 5.8 collective-permute-start
  83.9 5.8 collective-permute-start
  109.5 6.4 collective-permute-start
  116.6 7.9 %collective-permute-start = (f32[125,128]{1,0:T(8,128)}, f32[125,128]{1,0:T(8,128)S(1)}, u32[]{:S(2)}, u32[]{:S(2)}) collective-permute-start(f32[125,128]{1,0:T(8,128)} %get-tuple-element.491), channel_id=1, source_target_pairs={{0,16},{16,32},{32,48},{48,64},{64,80},{80,96},{96,112},{112,128},... | collective-permute-start | bytes 192008 | tf_op jit(solution)/shard_map/while/body/eval_jaxpr/ppermute | solution.py:16
  125.1 7.9 %collective-permute-start = (f32[125,128]{1,0:T(8,128)}, f32[125,128]{1,0:T(8,128)S(1)}, u32[]{:S(2)}, u32[]{:S(2)}) collective-permute-start(f32[125,128]{1,0:T(8,128)} %get-tuple-element.491), channel_id=1, source_target_pairs={{0,16},{16,32},{32,48},{48,64},{64,80},{80,96},{96,112},{112,128},... | collective-permute-start | bytes 192008 | tf_op jit(solution)/shard_map/while/body/eval_jaxpr/ppermute | solution.py:16
  133.6 193.5 %collective-permute-start = (f32[125,128]{1,0:T(8,128)}, f32[125,128]{1,0:T(8,128)S(1)}, u32[]{:S(2)}, u32[]{:S(2)}) collective-permute-start(f32[125,128]{1,0:T(8,128)} %get-tuple-element.491), channel_id=1, source_target_pairs={{0,16},{16,32},{32,48},{48,64},{64,80},{80,96},{96,112},{112,128},... | collective-permute-start | bytes 192008 | tf_op jit(solution)/shard_map/while/body/eval_jaxpr/ppermute | solution.py:16
  342.5 7.6 %collective-permute-start = (f32[125,128]{1,0:T(8,128)}, f32[125,128]{1,0:T(8,128)S(1)}, u32[]{:S(2)}, u32[]{:S(2)}) collective-permute-start(f32[125,128]{1,0:T(8,128)} %get-tuple-element.491), channel_id=1, source_target_pairs={{0,16},{16,32},{32,48},{48,64},{64,80},{80,96},{96,112},{112,128},... | collective-permute-start | bytes 192008 | tf_op jit(solution)/shard_map/while/body/eval_jaxpr/ppermute | solution.py:16
  365.4 8.1 %collective-permute-start = (f32[125,128]{1,0:T(8,128)}, f32[125,128]{1,0:T(8,128)S(1)}, u32[]{:S(2)}, u32[]{:S(2)}) collective-permute-start(f32[125,128]{1,0:T(8,128)} %get-tuple-element.491), channel_id=1, source_target_pairs={{0,16},{16,32},{32,48},{48,64},{64,80},{80,96},{96,112},{112,128},... | collective-permute-start | bytes 192008 | tf_op jit(solution)/shard_map/while/body/eval_jaxpr/ppermute | solution.py:16
  388.9 7.9 %collective-permute-start = (f32[125,128]{1,0:T(8,128)}, f32[125,128]{1,0:T(8,128)S(1)}, u32[]{:S(2)}, u32[]{:S(2)}) collective-permute-start(f32[125,128]{1,0:T(8,128)} %get-tuple-element.491), channel_id=1, source_target_pairs={{0,16},{16,32},{32,48},{48,64},{64,80},{80,96},{96,112},{112,128},... | collective-permute-start | bytes 192008 | tf_op jit(solution)/shard_map/while/body/eval_jaxpr/ppermute | solution.py:16
  417.1 12.0 %collective-permute-start.4 = (f32[2,125,512]{2,1,0:T(8,128)}, f32[2,125,512]{2,1,0:T(8,128)}, u32[]{:S(2)}, u32[]{:S(2)}) collective-permute-start(f32[2,125,512]{2,1,0:T(8,128)} %copy.19), channel_id=1, source_target_pairs={{0,1},{1,2},{2,3},{3,4},{4,5},{5,6},{6,7},{7,8},{8,9},{9,10},{10,1... | collective-permute-start | bytes 1536008 | tf_op jit(solution)/shard_map/ppermute | solution.py:21
  418.0 14.6 %collective-permute-start.5 = (f32[2,125,512]{2,1,0:T(8,128)}, f32[2,125,512]{2,1,0:T(8,128)}, u32[]{:S(2)}, u32[]{:S(2)}) collective-permute-start(f32[2,125,512]{2,1,0:T(8,128)} %copy.20), channel_id=1, source_target_pairs={{0,15},{1,0},{2,1},{3,2},{4,3},{5,4},{6,5},{7,6},{8,7},{9,8},{10,9... | collective-permute-start | bytes 1536008 | tf_op jit(solution)/shard_map/ppermute | solution.py:21
  466.8 5.8 collective-permute-start.1
  473.3 5.8 collective-permute-start.1
  479.7 5.8 collective-permute-start.1
  530.9 106.9 %collective-permute-start.1 = (f32[125,128]{1,0:T(8,128)}, f32[125,128]{1,0:T(8,128)S(1)}, u32[]{:S(2)}, u32[]{:S(2)}) collective-permute-start(f32[125,128]{1,0:T(8,128)} %get-tuple-element.521), channel_id=1, source_target_pairs={{0,16},{16,32},{32,48},{48,64},{64,80},{80,96},{96,112},{112,128},... | collective-permute-start | bytes 192008 | tf_op jit(solution)/shard_map/while/body/eval_jaxpr/ppermute | solution.py:16
  653.2 7.6 %collective-permute-start.1 = (f32[125,128]{1,0:T(8,128)}, f32[125,128]{1,0:T(8,128)S(1)}, u32[]{:S(2)}, u32[]{:S(2)}) collective-permute-start(f32[125,128]{1,0:T(8,128)} %get-tuple-element.521), channel_id=1, source_target_pairs={{0,16},{16,32},{32,48},{48,64},{64,80},{80,96},{96,112},{112,128},... | collective-permute-start | bytes 192008 | tf_op jit(solution)/shard_map/while/body/eval_jaxpr/ppermute | solution.py:16
  676.1 8.1 %collective-permute-start.1 = (f32[125,128]{1,0:T(8,128)}, f32[125,128]{1,0:T(8,128)S(1)}, u32[]{:S(2)}, u32[]{:S(2)}) collective-permute-start(f32[125,128]{1,0:T(8,128)} %get-tuple-element.521), channel_id=1, source_target_pairs={{0,16},{16,32},{32,48},{48,64},{64,80},{80,96},{96,112},{112,128},... | collective-permute-start | bytes 192008 | tf_op jit(solution)/shard_map/while/body/eval_jaxpr/ppermute | solution.py:16
  699.6 7.9 %collective-permute-start.1 = (f32[125,128]{1,0:T(8,128)}, f32[125,128]{1,0:T(8,128)S(1)}, u32[]{:S(2)}, u32[]{:S(2)}) collective-permute-start(f32[125,128]{1,0:T(8,128)} %get-tuple-element.521), channel_id=1, source_target_pairs={{0,16},{16,32},{32,48},{48,64},{64,80},{80,96},{96,112},{112,128},... | collective-permute-start | bytes 192008 | tf_op jit(solution)/shard_map/while/body/eval_jaxpr/ppermute | solution.py:16
  (40 other events, 190.7 us)
where the time goes:
time: 731 us; the launch traced here: 729 us
  waiting for transfers between devices  485 us (66%)
  local copies, waits for them, and re-layouts  97 us (13%)
  matrix products  77.2 us (11%)
  starting transfers between devices  60.9 us (8%)
  other arithmetic  7.71 us (1%)
    ppermute x38, waiting for transfers between devices, passed_along(): return lax.ppermute(shard, axis, pairs)  470 us
    dot_general x32, matrix products, product(): jnp.dot(matrix, vectors, precision=lax.Precision.HIGHEST, preferred_eleme...  60.2 us
    ppermute x38, starting transfers between devices, passed_along(): return lax.ppermute(shard, axis, pairs)  48.6 us
    reshape x16, local copies, waits for them, and re-layouts, face_grid(): return field.reshape(leading + (VARS, NODE, NODE, NODE, field.shape[-1]))  29.4 us
    another operation x34, local copies, waits for them, and re-layouts  23.6 us
    cond x48, local copies, waits for them, and re-layouts  20.1 us
    dot_general x4, matrix products, batched_product(): jnp.einsum('eab,ebr->ear', matrix, vectors, precision=lax.Precision.HIGHEST)  17 us
    ppermute x4, waiting for transfers between devices, from_behind(): lax.ppermute(shard, axis, [(i, (i + by) % count) for i in range(count)])  15.1 us
  transfers between devices with their start and end apart: 42, of which 40 were waited for; matrix products, arithmetic and copies ran while one was open for 1% of the time, Pallas kernels for 0%

commit v1 on v0

v1 whole, which is shorter than its diff:
```python
import jax
import jax.numpy as jnp
from jax import lax
from jax.experimental import pallas as pl
from jax.experimental.pallas import tpu as pltpu
from jax.sharding import PartitionSpec as P

VARS = 5
NODE = 5
UNK = 625
FACE = 125
F = 128
U = 640
W = 128
NP = 4
NQ = 2 * NP
RING = 4
MESH = pl.DeviceIdType.MESH
f32 = jnp.float32
bf16 = jnp.bfloat16


def dot(a, b):
    return jnp.dot(a, b, preferred_element_type=f32)


def halves(x):
    hi = x.astype(bf16)
    lo = (x - hi.astype(f32)).astype(bf16)
    return hi, lo


def left3(x):
    hi, lo = halves(x)
    return jnp.concatenate([hi, lo, hi], axis=1)


def right3(x):
    hi, lo = halves(x)
    return jnp.concatenate([hi, hi, lo], axis=0)


def product(a, b):
    return dot(left3(a), right3(b))


def kernel(
    faces, b_in, snu_in, f_in,
    out,
    bst, snust, fst, sh, sl, fh, fl, dbst, dfull, bfp, bsn3, bu3, hst, hsn3, hu3, hlf,
    gsn3, dsn3, m3, gf, g0f, phi, phik, coef, ca3, e3, phi3,
    sn, xq, gown, gpar, g0c, g0v, ag, xs, xb, tp, tin, ts, zs, hb, ob,
    load_sem, out_sem, zsend, zrecv, gsend, grecv, asend, arecv, xsend, xrecv, tsend, trecv,
    psend, precv, ksend, krecv,
):
    p = lax.axis_index("sweep")
    j = lax.axis_index("span")
    span = 16
    core = lax.rem(p, 2)
    chip = p // 2
    y = lax.rem(chip, RING)
    x = chip // RING
    mate = p + 1 - 2 * core
    up = lax.rem(j + 1, span)
    down = lax.rem(j + span - 1, span)

    def ring_peer(d):
        return (x * RING + lax.rem(y + d, RING)) * 2 + core

    over = lax.rem(p + 8, 16)

    loads = [
        pltpu.make_async_copy(b_in, bst, load_sem.at[0]),
        pltpu.make_async_copy(snu_in, snust, load_sem.at[1]),
        pltpu.make_async_copy(f_in, fst, load_sem.at[2]),
    ]
    for c in loads:
        c.start()

    barrier = pltpu.get_barrier_semaphore()
    for dev in ({"span": up}, {"span": down}, {"sweep": mate}, {"sweep": over},
                {"sweep": ring_peer(1)}, {"sweep": ring_peer(2)}, {"sweep": ring_peer(3)}):
        pl.semaphore_signal(barrier, inc=1, device_id=dev, device_id_type=MESH)
    pl.semaphore_wait(barrier, 7)

    def remote(src, dst, ss, rs, dev):
        return pltpu.make_async_remote_copy(
            src_ref=src, dst_ref=dst, send_sem=ss, recv_sem=rs, device_id=dev, device_id_type=MESH
        )

    def zdev(way):
        return {"span": up if way == 0 else down}

    def zcopy1(c, way):
        return remote(faces.at[way, c], sn.at[c, way], zsend.at[c, way], zrecv.at[c, way], zdev(way))

    def zcopy2(q, way):
        c = lax.rem(q, NP)
        return remote(zs.at[c, way], sn.at[q, way], zsend.at[q, way], zrecv.at[q, way], zdev(way))

    for c in range(NP):
        for way in range(2):
            zcopy1(c, way).start()

    def gcopy(q):
        return remote(gown.at[q], gpar.at[q], gsend.at[q], grecv.at[q], {"sweep": mate})

    def acopy(q, d):
        return remote(ag.at[q, y], ag.at[q, y], asend.at[q, d - 1], arecv.at[q, y], {"sweep": ring_peer(d)})

    def aland(q, d):
        k = lax.rem(y + RING - d, RING)
        return remote(ag.at[q, k], ag.at[q, k], asend.at[q, d - 1], arecv.at[q, k], {"sweep": ring_peer(d)})

    def xcopy(q):
        return remote(xs.at[q], xb.at[q], xsend.at[q], xrecv.at[q], {"sweep": over})

    def tcopy(q):
        return remote(ts.at[q], tin.at[q], tsend.at[q], trecv.at[q], {"sweep": mate})

    def pcopy():
        return remote(phi.at[core], phi.at[core], psend, precv, {"sweep": mate})

    def kcopy(d):
        return remote(phik.at[y], phik.at[y], ksend.at[d - 1], krecv.at[y], {"sweep": ring_peer(d)})

    def kland(d):
        k = lax.rem(y + RING - d, RING)
        return remote(phik.at[k], phik.at[k], ksend.at[d - 1], krecv.at[k], {"sweep": ring_peer(d)})

    loads[0].wait()
    loads[1].wait()
    for e in range(2):
        dbst[e, FACE:, :] = jnp.zeros((F - FACE, U), f32)
        for v in range(VARS):
            dbst[e, 25 * v:25 * v + 25, :] = bst[e, 125 * v + 100:125 * v + 125, :]
        hi, lo = halves(snust[e])
        sh[e] = hi
        sl[e] = lo
    dsnu = []
    dbs = []
    for e in range(2):
        hi, lo = halves(dbst[e])
        dbs.append((hi, lo))
        dsnu.append(dot(hi, sh[e]) + dot(hi, sl[e]) + dot(lo, sh[e]))
    m0 = dsnu[0][:, 2 * F:]
    m1 = dsnu[1][:, 2 * F:]
    m3[0] = left3(m0)
    m3[1] = left3(m1)
    dsn3[...] = left3(dsnu[0][:, :2 * F])
    gsn3[:, :6 * F] = left3(-dot(m3[1], right3(dsnu[0][:, :2 * F])))
    gsn3[:, 6 * F:] = left3(dsnu[1][:, :2 * F])
    phi[core] = dot(m3[1], right3(m0))
    pcopy().start()
    loads[2].wait()
    for e in range(2):
        hi, lo = halves(fst[e])
        fh[e] = hi
        fl[e] = lo
    df = []
    for e in range(2):
        hi, lo = dbs[e]
        df.append(dot(hi, fh[e]) + dot(hi, fl[e]) + dot(lo, fh[e]))
    gall = df[1] - dot(m3[1], right3(df[0]))
    for c in range(NP):
        g0f[c] = df[0][:, W * c:W * c + W]
        gf[c] = gall[:, W * c:W * c + W]
    pcopy().wait_recv()
    phi3[0] = left3(phi[0])
    phi3[1] = left3(phi[1])
    phik[y] = dot(phi3[1], right3(phi[0]))
    for d in (1, 2, 3):
        kcopy(d).start()

    def blocks():
        def one(n, _):
            e = n // 4
            rows = pl.ds(pl.multiple_of(lax.rem(n, 4) * 160, 160), 160)
            hi, lo = halves(bst[e, rows, :])
            r = dot(hi, sh[e]) + dot(hi, sl[e]) + dot(lo, sh[e])
            dfull[e, rows, :] = r
            bsn3[e, rows, :] = left3(r[:, :2 * F])
            bu3[e, rows, :] = left3(r[:, 2 * F:])
            r = dot(hi, fh[e]) + dot(hi, fl[e]) + dot(lo, fh[e])
            for c in range(NP):
                bfp[c, e, rows, :] = r[:, W * c:W * c + W]
            return 0

        lax.fori_loop(0, 8, one, 0)

    def face_rows():
        hst[FACE:F, :] = jnp.zeros((F - FACE, 3 * F), f32)
        hst[F + FACE:, :] = jnp.zeros((F - FACE, 3 * F), f32)

        def one(e, _):
            for g in range(25):
                hst[5 * g:5 * g + 5, :] = dfull[e, 25 * g + 20:25 * g + 25, :]
                hst[F + 5 * g:F + 5 * g + 5, :] = dfull[e, 25 * g:25 * g + 5, :]
            hsn3[e] = left3(hst[:, :2 * F])
            hu3[e] = left3(hst[:, 2 * F:])
            return 0

        lax.fori_loop(0, 2, one, 0)

        def two(n, _):
            c = n // 2
            e = lax.rem(n, 2)
            hlf[c, e, FACE:F, :] = jnp.zeros((F - FACE, W), f32)
            hlf[c, e, F + FACE:, :] = jnp.zeros((F - FACE, W), f32)
            for g in range(25):
                hlf[c, e, 5 * g:5 * g + 5, :] = bfp[c, e, 25 * g + 20:25 * g + 25, :]
                hlf[c, e, F + 5 * g:F + 5 * g + 5, :] = bfp[c, e, 25 * g:25 * g + 5, :]
            return 0

        lax.fori_loop(0, 2 * NP, two, 0)

    def coefficients():
        for d in (1, 2, 3):
            kland(d).wait_recv()
        eye = (lax.broadcasted_iota(jnp.int32, (F, F), 0) == lax.broadcasted_iota(jnp.int32, (F, F), 1)).astype(f32)
        coef[0] = eye
        coef[1] = eye

        def one(n, _):
            k = RING - 1 - n
            r = coef[0]
            s = coef[1]
            zero = jnp.zeros((F, F), f32)
            before = k < y
            a = jnp.where(before, r, zero)
            both = dot(left3(jnp.concatenate([r, s], axis=0)), right3(phik[k]))
            coef[0] = jnp.where(before, both[:F], r)
            coef[1] = both[F:]
            ua = dot(phi3[0], right3(a))
            col = pl.ds(pl.multiple_of(k * 3 * F, 3 * F), 3 * F)
            ca3[:, col] = left3(jnp.concatenate([a, ua, s], axis=0))
            return 0

        lax.fori_loop(0, RING, one, 0)
        e_map = coef[0]
        e3[:F, :] = left3(e_map)
        e3[F:, :] = left3(dot(phi3[0], right3(e_map)))

    def trace_in(q, c, lead):
        for way in range(2):
            zcopy2(q, way).wait_recv()
        for e in range(2):
            xq[q, e] = right3(jnp.concatenate([sn[q, 0, e], sn[q, 1, e]], axis=0))
        x0 = xq[q, 0]
        gown[q] = gf[c] - dot(gsn3[...], jnp.concatenate([x0, xq[q, 1]], axis=0))

        @pl.when(jnp.logical_not(lead))
        def _():
            gcopy(q).start()

        g0v[q] = g0f[c] - dot(dsn3[...], x0)

    def pair_up(q, c, lead):
        @pl.when(lead)
        def _():
            gcopy(q).wait_recv()
            own = gown[q]
            other = gpar[q]
            first = jnp.where(core == 0, own, other)
            second = jnp.where(core == 0, other, own)
            g0c[q] = first
            ag[q, y] = second + dot(phi3[1], right3(first))
            for d in (1, 2, 3):
                acopy(q, d).start()

    def settle(q, here, after):
        tin[q] = jnp.where(core == 0, here, after)
        ts[q] = jnp.where(core == 0, after, here)
        tcopy(q).start()

    def ring_sum(q, c, lead):
        @pl.when(lead)
        def _():
            for d in (1, 2, 3):
                aland(q, d).wait_recv()
            stack = jnp.concatenate([right3(ag[q, k]) for k in range(RING)], axis=0)
            r = dot(ca3[...], stack)

            @pl.when(x == 0)
            def _():
                xs[q] = r[2 * F:]
                xcopy(q).start()
                settle(q, r[:F], r[F:2 * F] + g0c[q])

            @pl.when(x == 1)
            def _():
                tp[q, 0] = r[:F]
                tp[q, 1] = r[F:2 * F] + g0c[q]

    def cross(q, c, lead):
        @pl.when(jnp.logical_and(lead, x == 1))
        def _():
            xcopy(q).wait_recv()
            r = dot(e3[...], right3(xb[q]))
            settle(q, tp[q, 0] + r[:F], tp[q, 1] + r[F:])

    def base(q, c, lead):
        @pl.when(q < NP)
        def _():
            for e in range(2):
                hb[c, e] = hlf[c, e] - dot(hsn3[e], xq[q, e])

        @pl.when(q >= NP)
        def _():
            for e in range(2):
                ob[c, e] = bfp[c, e, :UNK, :] - dot(bsn3[e], xq[q, e])[:UNK]

    def out_copy(c):
        return pltpu.make_async_copy(
            ob.at[c], out.at[:, :, pl.ds(pl.multiple_of(c * W, W), W)], out_sem.at[c]
        )

    def finish(q, c, lead):
        @pl.when(jnp.logical_not(lead))
        def _():
            tcopy(q).wait_recv()

        t0 = right3(tin[q])
        t1 = right3(g0v[q] - dot(m3[0], t0))

        @pl.when(q < NP)
        def _():
            for e, t in ((0, t0), (1, t1)):
                h = hb[c, e] - dot(hu3[e], t)
                zs[c, 0, e] = h[:F]
                zs[c, 1, e] = h[F:]
            for way in range(2):
                zcopy2(q + NP, way).start()

        @pl.when(q >= NP)
        def _():
            for e, t in ((0, t0), (1, t1)):
                ob[c, e] = ob[c, e] - dot(bu3[e], t)[:UNK]
            out_copy(c).start()

    gap = 6

    def slot(k, _):
        def at(behind, stage):
            n = k - behind
            active = jnp.logical_or(
                jnp.logical_and(n >= 0, n < NP), jnp.logical_and(n >= gap, n < gap + NP)
            )

            @pl.when(active)
            def _():
                late = (n >= gap).astype(jnp.int32)
                c = n - gap * late
                q = c + NP * late
                stage(q, c, core == lax.rem(c, 2))

        at(4, finish)
        at(3, cross)

        @pl.when(k == 2)
        def _():
            coefficients()

        at(2, ring_sum)
        at(2, base)
        at(1, pair_up)
        at(0, trace_in)

        @pl.when(k == 0)
        def _():
            blocks()

        @pl.when(k == 1)
        def _():
            face_rows()

        return 0

    lax.fori_loop(0, gap + NP + 4, slot, 0)

    pcopy().wait_send()
    for d in (1, 2, 3):
        kcopy(d).wait_send()

    def drain(q, _):
        for way in range(2):
            zcopy2(q, way).wait_send()
        lead = core == lax.rem(q, 2)

        @pl.when(lead)
        def _():
            for d in (1, 2, 3):
                acopy(q, d).wait_send()
            tcopy(q).wait_send()

            @pl.when(x == 0)
            def _():
                xcopy(q).wait_send()

        @pl.when(jnp.logical_not(lead))
        def _():
            gcopy(q).wait_send()

        return 0

    lax.fori_loop(0, NQ, drain, 0)
    for c in range(NP):
        out_copy(c).wait()


def solve(faces, b, snu, f):
    V = pltpu.VMEM
    D = pltpu.SemaphoreType.DMA
    scratch = [
        V((2, U, U), f32), V((2, U, 3 * F), f32), V((2, U, 512), f32),
        V((2, U, 3 * F), bf16), V((2, U, 3 * F), bf16),
        V((2, U, 512), bf16), V((2, U, 512), bf16), V((2, F, U), f32), V((2, U, 3 * F), f32),
        V((NP, 2, U, W), f32), V((2, U, 6 * F), bf16), V((2, U, 3 * F), bf16),
        V((2 * F, 3 * F), f32), V((2, 2 * F, 6 * F), bf16), V((2, 2 * F, 3 * F), bf16),
        V((NP, 2, 2 * F, W), f32),
        V((F, 12 * F), bf16), V((F, 6 * F), bf16), V((2, F, 3 * F), bf16), V((NP, F, W), f32),
        V((NP, F, W), f32), V((2, F, F), f32), V((RING, F, F), f32), V((2, F, F), f32),
        V((3 * F, 12 * F), bf16), V((2 * F, 3 * F), bf16), V((2, F, 3 * F), bf16),
        V((NQ, 2, 2, F, W), f32), V((NQ, 2, 6 * F, W), bf16), V((NQ, F, W), f32), V((NQ, F, W), f32),
        V((NQ, F, W), f32), V((NQ, F, W), f32), V((NQ, RING, F, W), f32), V((NQ, F, W), f32),
        V((NQ, F, W), f32), V((NQ, 2, F, W), f32), V((NQ, F, W), f32), V((NQ, F, W), f32),
        V((NP, 2, 2, F, W), f32), V((NP, 2, 2 * F, W), f32), V((NP, 2, UNK, W), f32),
        D((3,)), D((NP,)), D((NQ, 2)), D((NQ, 2)), D((NQ,)), D((NQ,)), D((NQ, 3)), D((NQ, RING)),
        D((NQ,)), D((NQ,)), D((NQ,)), D((NQ,)), D, D, D((3,)), D((RING,)),
    ]
    any_spec = pl.BlockSpec(memory_space=pl.ANY)
    return pl.pallas_call(
        kernel,
        out_shape=jax.ShapeDtypeStruct((2, UNK, 512), f32),
        in_specs=[any_spec] * 4,
        out_specs=any_spec,
        scratch_shapes=scratch,
        compiler_params=pltpu.CompilerParams(
            collective_id=0, has_side_effects=True, vmem_limit_bytes=60 * 1024 * 1024
        ),
    )(faces, b, snu, f)


def per_device(right_side, start_field, block_inverse, upwind_block, south_block, north_block):
    rows = (0, U - UNK)
    cols = (0, F - FACE)
    none = (0, 0)
    b = jnp.pad(block_inverse[:, 0], (none, rows, rows))
    parts = [jnp.pad(m[:, 0], (none, rows, cols)) for m in (south_block, north_block, upwind_block)]
    snu = jnp.concatenate(parts, axis=2)
    f = jnp.pad(right_side[:, 0], (none, rows, none))
    grid = start_field[:, 0].reshape(2, VARS * NODE, NODE, NODE, NP, W)
    faces = jnp.stack([grid[:, :, NODE - 1], grid[:, :, 0]])
    faces = jnp.transpose(faces.reshape(2, 2, FACE, NP, W), (0, 3, 1, 2, 4))
    faces = jnp.pad(faces, (none, none, none, cols, none))
    return solve(faces, b, snu, f)[:, None]


def solution(mesh):
    spec = P("sweep", "span", None, None)
    return jax.shard_map(
        per_device, mesh=mesh, in_specs=(spec,) * 6, out_specs=spec, check_vma=False
    )
```

time: 731 us -> 87.8 us (0.12)
  the two profiles are of different devices: /device:TPU:27 before, /device:TPU:6 now
where the time goes in v1:
time: 87.8 us; the launch traced here: 86.1 us
  Pallas kernels  68.5 us (78%)
  local copies, waits for them, and re-layouts  16 us (18%)
  other arithmetic  1.52 us (2%)
    pallas_call x1, Pallas kernels, solve(): pl.pallas_call(kernel, out_shape=jax.ShapeDtypeStruct((2, UNK, 512), f32)...  68.5 us
    broadcast_in_dim x1, local copies, waits for them, and re-layouts, per_device(): return solve(faces, b, snu, f)[:, None]  5.83 us
    unnamed x10, local copies, waits for them, and re-layouts  3.98 us
    pad x1, local copies, waits for them, and re-layouts, per_device(): b = jnp.pad(block_inverse[:, 0], (none, rows, rows))  1.88 us

profile of v1, /device:TPU:6, one launch (start us, length us, event | category | flops | bytes accessed | tf_op | source)
XLA Modules:
  0.0 86.1 jit_solution(4198693147252985369)
XLA Ops:
  0.0 0.0 copy-start.2
  0.0 1.4 %copy_bitcast_fusion.2 = (f32[2,625,125]{2,1,0:T(8,128)S(1)}, f32[2,625,125]{2,1,0:T(8,128)S(1)}) fusion(f32[2,1,625,125]{3,1,2,0:T(1,128)} %param.9, f32[2,1,625,125]{3,1,2,0:T(1,128)} %param.11), kind=kLoop, calls=%fused_computation.10 | loop fusion | bytes 2500000
  1.4 0.0 copy-done.2
  1.5 1.4 %select_maximum_fusion.snu_in = f32[2,640,384]{2,1,0:T(8,128)} fusion(f32[2,625,125]{2,1,0:T(8,128)S(1)} %get-tuple-element.7, f32[2,625,125]{2,1,0:T(8,128)S(1)} %get-tuple-element.8, f32[2,625,125]{2,1,0:T(8,128)S(1)} %bitcast.26), kind=kLoop, calls=%fused_computation.4 | loop fusion | flops 4915200 | bytes 3841080 | tf_op jit(solution)/shard_map/concatenate | solution.py:450
  2.9 1.3 %fusion.1 = (f32[2,25,1,5,4,128]{5,4,3,2,1,0:T(4,128)S(1)}, f32[2,25,1,5,4,128]{5,4,3,2,1,0:T(4,128)S(1)}) fusion(f32[2,25,5,5,4,128]{5,4,3,2,1,0:T(4,128)} %bitcast.29), kind=kLoop, calls=%fused_computation.13 | loop fusion | bytes 2048000 | tf_op jit(solution)/shard_map/slice | solution.py:453
  4.3 0.0 copy-start
  4.3 0.1 maximum_bitcast_fusion
  4.4 1.2 %pad.22.faces = f32[2,4,2,128,128]{4,3,2,1,0:T(8,128)} pad(f32[2,4,2,125,128]{4,3,2,1,0:T(8,128)S(1)} %maximum_bitcast_fusion, f32[]{:T(128)} %constant.2.clone.1), padding=0_0x0_0x0_0x0_3x0_0 | pad | bytes 2072580 | tf_op jit(solution)/shard_map/jit(_pad)/pad | solution.py:455
  5.6 1.0 %copy-done = f32[2,1,625,625]{3,1,2,0:T(1,128)S(1)} copy-done((f32[2,1,625,625]{3,1,2,0:T(1,128)S(1)}, f32[2,1,625,625]{3,1,2,0:T(1,128)}, u32[]{:S(2)}) %copy-start) | copy-done | bytes 3125024
  6.6 0.2 copy.27
  6.8 0.0 copy-start.1
  6.8 1.9 %pad.23.b_in = f32[2,640,640]{2,1,0:T(8,128)} pad(f32[2,625,625]{2,1,0:T(8,128)S(1)} %bitcast.23, f32[]{:T(128)} %constant.2.clone.1), padding=0_0x0_15x0_15 | pad | bytes 6401804 | tf_op jit(solution)/shard_map/jit(_pad)/pad | solution.py:448
  8.7 1.0 %copy-done.1 = f32[2,1,625,512]{3,1,2,0:T(1,128)S(1)} copy-done((f32[2,1,625,512]{3,1,2,0:T(1,128)S(1)}, f32[2,1,625,512]{3,1,2,0:T(1,128)}, u32[]{:S(2)}) %copy-start.1) | copy-done | bytes 2560024
  9.7 0.2 copy.28
  10.0 1.7 %pad.27.f_in = f32[2,640,512]{2,1,0:T(8,128)} pad(f32[2,625,512]{2,1,0:T(8,128)S(1)} %bitcast.24, f32[]{:T(128)} %constant.2.clone.1), padding=0_0x0_15x0_0 | pad | bytes 5181444 | tf_op jit(solution)/shard_map/jit(_pad)/pad | solution.py:451
  11.7 68.5 %shard_map.64 = f32[2,625,512]{2,1,0:T(8,128)} custom-call(f32[2,4,2,128,128]{4,3,2,1,0:T(8,128)} %pad.22.faces, f32[2,640,640]{2,1,0:T(8,128)} %pad.23.b_in, f32[2,640,384]{2,1,0:T(8,128)} %select_maximum_fusion.snu_in, f32[2,640,512]{2,1,0:T(8,128)} %pad.27.f_in), custom_call_target="tpu_custom_call" | custom-call | tf_op jit(solution)/shard_map/pallas_call | solution.py:432
  80.2 5.8 %copy.14 = f32[2,1,625,512]{3,1,2,0:T(1,128)} copy(f32[2,1,625,512]{3,2,0,1:T(8,128)} %bitcast.25) | data formatting | bytes 5120000 | tf_op jit(solution)/shard_map/broadcast_in_dim | solution.py:456
  (3 shorter events, 0.1 us)
Async XLA Ops:
  0.0 1.5 %copy-start.2 = (f32[2,1,625,125]{3,1,2,0:T(1,128)S(1)}, f32[2,1,625,125]{3,1,2,0:T(1,128)}, u32[]{:S(2)}) copy-start(f32[2,1,625,125]{3,1,2,0:T(1,128)} %param.10) | copy-start | bytes 1875004
  4.3 2.3 %copy-start = (f32[2,1,625,625]{3,1,2,0:T(1,128)S(1)}, f32[2,1,625,625]{3,1,2,0:T(1,128)}, u32[]{:S(2)}) copy-start(f32[2,1,625,625]{3,1,2,0:T(1,128)} %param.8) | copy-start | bytes 9375004
  6.8 2.9 %copy-start.1 = (f32[2,1,625,512]{3,1,2,0:T(1,128)S(1)}, f32[2,1,625,512]{3,1,2,0:T(1,128)}, u32[]{:S(2)}) copy-start(f32[2,1,625,512]{3,1,2,0:T(1,128)} %param.6) | copy-start | bytes 7680004

commit v2 on v1

--- a/solution.py
+++ b/solution.py
@@ -45,9 +45,9 @@
 
 
 def kernel(
-    faces, b_in, snu_in, f_in,
+    start, b_in, s_in, n_in, u_in, f_in,
     out,
-    bst, snust, fst, sh, sl, fh, fl, dbst, dfull, bfp, bsn3, bu3, hst, hsn3, hu3, hlf,
+    bst, sust, fst, sh, sl, fh, fl, dbst, hbst, bch, bcl, bfp, bsn3, bu3, hsn3, hu3, hlf, snr,
     gsn3, dsn3, m3, gf, g0f, phi, phik, coef, ca3, e3, phi3,
     sn, xq, gown, gpar, g0c, g0v, ag, xs, xb, tp, tin, ts, zs, hb, ob,
     load_sem, out_sem, zsend, zrecv, gsend, grecv, asend, arecv, xsend, xrecv, tsend, trecv,
@@ -69,13 +69,8 @@
 
     over = lax.rem(p + 8, 16)
 
-    loads = [
-        pltpu.make_async_copy(b_in, bst, load_sem.at[0]),
-        pltpu.make_async_copy(snu_in, snust, load_sem.at[1]),
-        pltpu.make_async_copy(f_in, fst, load_sem.at[2]),
-    ]
-    for c in loads:
-        c.start()
+    def load(src, dst, n):
+        return pltpu.make_async_copy(src, dst, load_sem.at[n])
 
     barrier = pltpu.get_barrier_semaphore()
     for dev in ({"span": up}, {"span": down}, {"sweep": mate}, {"sweep": over},
@@ -92,7 +87,9 @@
         return {"span": up if way == 0 else down}
 
     def zcopy1(c, way):
-        return remote(faces.at[way, c], sn.at[c, way], zsend.at[c, way], zrecv.at[c, way], zdev(way))
+        level = NODE - 1 if way == 0 else 0
+        src = start.at[:, :, level, :, 0, pl.ds(pl.multiple_of(c * W, W), W)]
+        return remote(src, snr.at[c, way], zsend.at[c, way], zrecv.at[c, way], zdev(way))
 
     def zcopy2(q, way):
         c = lax.rem(q, NP)
@@ -101,7 +98,6 @@
     for c in range(NP):
         for way in range(2):
             zcopy1(c, way).start()
-
     def gcopy(q):
         return remote(gown.at[q], gpar.at[q], gsend.at[q], grecv.at[q], {"sweep": mate})
 
@@ -128,15 +124,38 @@
         k = lax.rem(y + RING - d, RING)
         return remote(phik.at[k], phik.at[k], ksend.at[d - 1], krecv.at[k], {"sweep": ring_peer(d)})
 
-    loads[0].wait()
-    loads[1].wait()
+    b_load = load(b_in.at[:, :, 0, :], bst, 0)
+    b_load.start()
+    su_loads = [load(m.at[:, :, 0, :], sust.at[n], 1 + n) for n, m in enumerate((s_in, n_in, u_in))]
+    for c in su_loads:
+        c.start()
+    f_load = load(f_in.at[:, :, 0, :], fst, 4)
+    f_load.start()
+
+    edge = pl.ds(U - F, F)
+    hbst[:, edge] = jnp.zeros((2 * F, F), f32)
+    hbst[FACE:F, :] = jnp.zeros((F - FACE, U), f32)
+    hbst[F + FACE:, :] = jnp.zeros((F - FACE, U), f32)
+    bch[:, edge] = jnp.zeros((160, F), bf16)
+    bcl[:, edge] = jnp.zeros((160, F), bf16)
     for e in range(2):
+        dbst[e, :, edge] = jnp.zeros((F, F), f32)
         dbst[e, FACE:, :] = jnp.zeros((F - FACE, U), f32)
+        for ref in (sh, sl):
+            ref[e] = jnp.zeros((U, 3 * F), bf16)
+        for ref in (fh, fl):
+            ref[e, U - 16:, :] = jnp.zeros((16, 512), bf16)
+
+    b_load.wait()
+    for e in range(2):
         for v in range(VARS):
-            dbst[e, 25 * v:25 * v + 25, :] = bst[e, 125 * v + 100:125 * v + 125, :]
-        hi, lo = halves(snust[e])
-        sh[e] = hi
-        sl[e] = lo
+            dbst[e, 25 * v:25 * v + 25, :UNK] = bst[e, 125 * v + 100:125 * v + 125, :]
+    for n in range(3):
+        su_loads[n].wait()
+        for e in range(2):
+            hi, lo = halves(sust[n, e])
+            sh[e, :UNK, F * n:F * n + FACE] = hi
+            sl[e, :UNK, F * n:F * n + FACE] = lo
     dsnu = []
     dbs = []
     for e in range(2):
@@ -152,11 +171,11 @@
     gsn3[:, 6 * F:] = left3(dsnu[1][:, :2 * F])
     phi[core] = dot(m3[1], right3(m0))
     pcopy().start()
-    loads[2].wait()
+    f_load.wait()
     for e in range(2):
         hi, lo = halves(fst[e])
-        fh[e] = hi
-        fl[e] = lo
+        fh[e, :UNK, :] = hi
+        fl[e, :UNK, :] = lo
     df = []
     for e in range(2):
         hi, lo = dbs[e]
@@ -172,13 +191,28 @@
     for d in (1, 2, 3):
         kcopy(d).start()
 
-    def blocks():
-        def one(n, _):
+    def blocks(start_at):
+        def one(i, _):
+            n = start_at + i
             e = n // 4
-            rows = pl.ds(pl.multiple_of(lax.rem(n, 4) * 160, 160), 160)
-            hi, lo = halves(bst[e, rows, :])
+            m = lax.rem(n, 4)
+            rows = pl.ds(pl.multiple_of(m * 160, 160), 160)
+
+            @pl.when(m < 3)
+            def _():
+                hi, lo = halves(bst[e, rows, :])
+                bch[:, :UNK] = hi
+                bcl[:, :UNK] = lo
+
+            @pl.when(m == 3)
+            def _():
+                hi, lo = halves(bst[e, 480:UNK, :])
+                bch[:UNK - 480, :UNK] = hi
+                bcl[:UNK - 480, :UNK] = lo
+
+            hi = bch[...]
+            lo = bcl[...]
             r = dot(hi, sh[e]) + dot(hi, sl[e]) + dot(lo, sh[e])
-            dfull[e, rows, :] = r
             bsn3[e, rows, :] = left3(r[:, :2 * F])
             bu3[e, rows, :] = left3(r[:, 2 * F:])
             r = dot(hi, fh[e]) + dot(hi, fl[e]) + dot(lo, fh[e])
@@ -186,33 +220,19 @@
                 bfp[c, e, rows, :] = r[:, W * c:W * c + W]
             return 0
 
-        lax.fori_loop(0, 8, one, 0)
-
-    def face_rows():
-        hst[FACE:F, :] = jnp.zeros((F - FACE, 3 * F), f32)
-        hst[F + FACE:, :] = jnp.zeros((F - FACE, 3 * F), f32)
-
-        def one(e, _):
-            for g in range(25):
-                hst[5 * g:5 * g + 5, :] = dfull[e, 25 * g + 20:25 * g + 25, :]
-                hst[F + 5 * g:F + 5 * g + 5, :] = dfull[e, 25 * g:25 * g + 5, :]
-            hsn3[e] = left3(hst[:, :2 * F])
-            hu3[e] = left3(hst[:, 2 * F:])
-            return 0
-
         lax.fori_loop(0, 2, one, 0)
 
-        def two(n, _):
-            c = n // 2
-            e = lax.rem(n, 2)
-            hlf[c, e, FACE:F, :] = jnp.zeros((F - FACE, W), f32)
-            hlf[c, e, F + FACE:, :] = jnp.zeros((F - FACE, W), f32)
-            for g in range(25):
-                hlf[c, e, 5 * g:5 * g + 5, :] = bfp[c, e, 25 * g + 20:25 * g + 25, :]
-                hlf[c, e, F + 5 * g:F + 5 * g + 5, :] = bfp[c, e, 25 * g:25 * g + 5, :]
-            return 0
-
-        lax.fori_loop(0, 2 * NP, two, 0)
+    def face_rows(e):
+        for g in range(25):
+            hbst[5 * g:5 * g + 5, :UNK] = bst[e, 25 * g + 20:25 * g + 25, :]
+            hbst[F + 5 * g:F + 5 * g + 5, :UNK] = bst[e, 25 * g:25 * g + 5, :]
+        hi, lo = halves(hbst[...])
+        r = dot(hi, sh[e]) + dot(hi, sl[e]) + dot(lo, sh[e])
+        hsn3[e] = left3(r[:, :2 * F])
+        hu3[e] = left3(r[:, 2 * F:])
+        r = dot(hi, fh[e]) + dot(hi, fl[e]) + dot(lo, fh[e])
+        for c in range(NP):
+            hlf[c, e] = r[:, W * c:W * c + W]
 
     def coefficients():
         for d in (1, 2, 3):
@@ -242,8 +262,20 @@
         e3[F:, :] = left3(dot(phi3[0], right3(e_map)))
 
     def trace_in(q, c, lead):
-        for way in range(2):
-            zcopy2(q, way).wait_recv()
+        @pl.when(q < NP)
+        def _():
+            for way in range(2):
+                zcopy1(c, way).wait_recv()
+                for e in range(2):
+                    sn[q, way, e, FACE:, :] = jnp.zeros((F - FACE, W), f32)
+                    for g in range(25):
+                        sn[q, way, e, 5 * g:5 * g + 5, :] = snr[c, way, e, g]
+
+        @pl.when(q >= NP)
+        def _():
+            for way in range(2):
+                zcopy2(q, way).wait_recv()
+
         for e in range(2):
             xq[q, e] = right3(jnp.concatenate([sn[q, 0, e], sn[q, 1, e]], axis=0))
         x0 = xq[q, 0]
@@ -299,12 +331,13 @@
             r = dot(e3[...], right3(xb[q]))
             settle(q, tp[q, 0] + r[:F], tp[q, 1] + r[F:])
 
-    def base(q, c, lead):
+    def base1(q, c, lead):
         @pl.when(q < NP)
         def _():
             for e in range(2):
                 hb[c, e] = hlf[c, e] - dot(hsn3[e], xq[q, e])
 
+    def base2(q, c, lead):
         @pl.when(q >= NP)
         def _():
             for e in range(2):
@@ -312,7 +345,7 @@
 
     def out_copy(c):
         return pltpu.make_async_copy(
-            ob.at[c], out.at[:, :, pl.ds(pl.multiple_of(c * W, W), W)], out_sem.at[c]
+            ob.at[c], out.at[:, :, 0, pl.ds(pl.multiple_of(c * W, W), W)], out_sem.at[c]
         )
 
     def finish(q, c, lead):
@@ -356,35 +389,37 @@
 
         at(4, finish)
         at(3, cross)
-
-        @pl.when(k == 2)
-        def _():
-            coefficients()
-
+        at(3, base1)
         at(2, ring_sum)
-        at(2, base)
+        at(2, base2)
         at(1, pair_up)
         at(0, trace_in)
 
-        @pl.when(k == 0)
-        def _():
-            blocks()
-
         @pl.when(k == 1)
         def _():
-            face_rows()
+            coefficients()
+
+        @pl.when(k < 2)
+        def _():
+            face_rows(k)
+
+        @pl.when(jnp.logical_and(k >= 4, k < 8))
+        def _():
+            blocks(2 * (k - 4))
 
         return 0
 
     lax.fori_loop(0, gap + NP + 4, slot, 0)
 
     pcopy().wait_send()
+    for c in range(NP):
+        for way in range(2):
+            zcopy1(c, way).wait_send()
+            zcopy2(c + NP, way).wait_send()
     for d in (1, 2, 3):
         kcopy(d).wait_send()
 
     def drain(q, _):
-        for way in range(2):
-            zcopy2(q, way).wait_send()
         lead = core == lax.rem(q, 2)
 
         @pl.when(lead)
@@ -408,16 +443,16 @@
         out_copy(c).wait()
 
 
-def solve(faces, b, snu, f):
+def solve(*args):
     V = pltpu.VMEM
     D = pltpu.SemaphoreType.DMA
     scratch = [
-        V((2, U, U), f32), V((2, U, 3 * F), f32), V((2, U, 512), f32),
-        V((2, U, 3 * F), bf16), V((2, U, 3 * F), bf16),
-        V((2, U, 512), bf16), V((2, U, 512), bf16), V((2, F, U), f32), V((2, U, 3 * F), f32),
+        V((2, UNK, UNK), f32), V((3, 2, UNK, FACE), f32), V((2, UNK, 512), f32),
+        V((2, U, 3 * F), bf16), V((2, U, 3 * F), bf16), V((2, U, 512), bf16), V((2, U, 512), bf16),
+        V((2, F, U), f32), V((2 * F, U), f32), V((160, U), bf16), V((160, U), bf16),
         V((NP, 2, U, W), f32), V((2, U, 6 * F), bf16), V((2, U, 3 * F), bf16),
-        V((2 * F, 3 * F), f32), V((2, 2 * F, 6 * F), bf16), V((2, 2 * F, 3 * F), bf16),
-        V((NP, 2, 2 * F, W), f32),
+        V((2, 2 * F, 6 * F), bf16), V((2, 2 * F, 3 * F), bf16), V((NP, 2, 2 * F, W), f32),
+        V((NP, 2, 2, 25, NODE, W), f32),
         V((F, 12 * F), bf16), V((F, 6 * F), bf16), V((2, F, 3 * F), bf16), V((NP, F, W), f32),
         V((NP, F, W), f32), V((2, F, F), f32), V((RING, F, F), f32), V((2, F, F), f32),
         V((3 * F, 12 * F), bf16), V((2 * F, 3 * F), bf16), V((2, F, 3 * F), bf16),
@@ -425,35 +460,29 @@
         V((NQ, F, W), f32), V((NQ, F, W), f32), V((NQ, RING, F, W), f32), V((NQ, F, W), f32),
         V((NQ, F, W), f32), V((NQ, 2, F, W), f32), V((NQ, F, W), f32), V((NQ, F, W), f32),
         V((NP, 2, 2, F, W), f32), V((NP, 2, 2 * F, W), f32), V((NP, 2, UNK, W), f32),
-        D((3,)), D((NP,)), D((NQ, 2)), D((NQ, 2)), D((NQ,)), D((NQ,)), D((NQ, 3)), D((NQ, RING)),
+        D((5,)), D((NP,)), D((NQ, 2)), D((NQ, 2)), D((NQ,)), D((NQ,)), D((NQ, 3)), D((NQ, RING)),
         D((NQ,)), D((NQ,)), D((NQ,)), D((NQ,)), D, D, D((3,)), D((RING,)),
     ]
     any_spec = pl.BlockSpec(memory_space=pl.ANY)
     return pl.pallas_call(
         kernel,
-        out_shape=jax.ShapeDtypeStruct((2, UNK, 512), f32),
-        in_specs=[any_spec] * 4,
+        out_shape=jax.ShapeDtypeStruct((2, UNK, 1, 512), f32),
+        in_specs=[any_spec] * 6,
         out_specs=any_spec,
         scratch_shapes=scratch,
         compiler_params=pltpu.CompilerParams(
             collective_id=0, has_side_effects=True, vmem_limit_bytes=60 * 1024 * 1024
         ),
-    )(faces, b, snu, f)
+    )(*args)
 
 
 def per_device(right_side, start_field, block_inverse, upwind_block, south_block, north_block):
-    rows = (0, U - UNK)
-    cols = (0, F - FACE)
-    none = (0, 0)
-    b = jnp.pad(block_inverse[:, 0], (none, rows, rows))
-    parts = [jnp.pad(m[:, 0], (none, rows, cols)) for m in (south_block, north_block, upwind_block)]
-    snu = jnp.concatenate(parts, axis=2)
-    f = jnp.pad(right_side[:, 0], (none, rows, none))
-    grid = start_field[:, 0].reshape(2, VARS * NODE, NODE, NODE, NP, W)
-    faces = jnp.stack([grid[:, :, NODE - 1], grid[:, :, 0]])
-    faces = jnp.transpose(faces.reshape(2, 2, FACE, NP, W), (0, 3, 1, 2, 4))
-    faces = jnp.pad(faces, (none, none, none, cols, none))
-    return solve(faces, b, snu, f)[:, None]
+    def rows_first(a):
+        return jnp.transpose(a, (0, 2, 1, 3))
+
+    grid = rows_first(start_field).reshape(2, VARS * NODE, NODE, NODE, 1, 512)
+    rest = [rows_first(a) for a in (block_inverse, south_block, north_block, upwind_block, right_side)]
+    return rows_first(solve(grid, *rest))
 
 
 def solution(mesh):

time: 87.8 us -> 69.6 us (0.79)
  the two profiles are of different devices: /device:TPU:6 before, /device:TPU:2 now
where the time goes in v2:
time: 69.6 us; the launch traced here: 69.5 us
  Pallas kernels  64.5 us (93%)
  local copies, waits for them, and re-layouts  4.95 us (7%)
    pallas_call x1, Pallas kernels, solve(): pl.pallas_call(kernel, out_shape=jax.ShapeDtypeStruct((2, UNK, 1, 512), f...  64.5 us
    unnamed x1, local copies, waits for them, and re-layouts  4.95 us

profile of v2, /device:TPU:2, one launch (start us, length us, event | category | flops | bytes accessed | tf_op | source)
XLA Modules:
  0.0 69.5 jit_solution(12547483552898884776)
XLA Ops:
  0.0 64.5 %shard_map.64 = f32[2,625,1,512]{3,2,1,0:T(1,128)} custom-call(f32[2,25,5,5,1,512]{5,4,3,2,1,0:T(1,128)} %bitcast.9, f32[2,625,1,625]{3,2,1,0:T(1,128)} %bitcast.8, f32[2,625,1,125]{3,2,1,0:T(1,128)} %bitcast.11, f32[2,625,1,125]{3,2,1,0:T(1,128)} %bitcast.12, f32[2,625,1,125]{3,2,1,0:T(1,128)} %bitcast.13, f32[2,625,1,512]{3,2,1,0:T(1,128)} %bitcast.10), custom_call_target="tpu_custom_call" | custom-call | tf_op jit(solution)/shard_map/pallas_call | solution.py:467
  64.5 4.9 %copy.8 = f32[2,1,625,512]{3,1,2,0:T(1,128)} copy(f32[2,1,625,512]{3,1,2,0:T(1,128)} %bitcast.7) | data formatting | bytes 5120000

commit v3 on v2

--- a/solution.py
+++ b/solution.py
@@ -220,7 +220,7 @@
                 bfp[c, e, rows, :] = r[:, W * c:W * c + W]
             return 0
 
-        lax.fori_loop(0, 2, one, 0)
+        lax.fori_loop(0, 1, one, 0)
 
     def face_rows(e):
         for g in range(25):
@@ -297,7 +297,7 @@
             second = jnp.where(core == 0, other, own)
             g0c[q] = first
             ag[q, y] = second + dot(phi3[1], right3(first))
-            for d in (1, 2, 3):
+            for d in (2, 1, 3):
                 acopy(q, d).start()
 
     def settle(q, here, after):
@@ -345,7 +345,7 @@
 
     def out_copy(c):
         return pltpu.make_async_copy(
-            ob.at[c], out.at[:, :, 0, pl.ds(pl.multiple_of(c * W, W), W)], out_sem.at[c]
+            ob.at[c], out.at[c], out_sem.at[c]
         )
 
     def finish(q, c, lead):
@@ -371,7 +371,7 @@
                 ob[c, e] = ob[c, e] - dot(bu3[e], t)[:UNK]
             out_copy(c).start()
 
-    gap = 6
+    gap = 7
 
     def slot(k, _):
         def at(behind, stage):
@@ -387,14 +387,13 @@
                 q = c + NP * late
                 stage(q, c, core == lax.rem(c, 2))
 
-        at(4, finish)
-        at(3, cross)
-        at(3, base1)
-        at(2, ring_sum)
-        at(2, base2)
+        at(5, finish)
+        at(4, cross)
+        at(4, base1)
+        at(3, ring_sum)
+        at(3, base2)
         at(1, pair_up)
         at(0, trace_in)
-
         @pl.when(k == 1)
         def _():
             coefficients()
@@ -403,13 +402,14 @@
         def _():
             face_rows(k)
 
-        @pl.when(jnp.logical_and(k >= 4, k < 8))
-        def _():
-            blocks(2 * (k - 4))
+        @pl.when(jnp.logical_and(k >= 2, k < 10))
+        def _():
+            blocks(k - 2)
+
 
         return 0
 
-    lax.fori_loop(0, gap + NP + 4, slot, 0)
+    lax.fori_loop(0, gap + NP + 5, slot, 0)
 
     pcopy().wait_send()
     for c in range(NP):
@@ -466,7 +466,7 @@
     any_spec = pl.BlockSpec(memory_space=pl.ANY)
     return pl.pallas_call(
         kernel,
-        out_shape=jax.ShapeDtypeStruct((2, UNK, 1, 512), f32),
+        out_shape=jax.ShapeDtypeStruct((NP, 2, UNK, W), f32),
         in_specs=[any_spec] * 6,
         out_specs=any_spec,
         scratch_shapes=scratch,
@@ -476,13 +476,41 @@
     )(*args)
 
 
+def write_out(panels, out, buf, load_sem, out_sem):
+    loads = [pltpu.make_async_copy(panels.at[c], buf.at[c], load_sem.at[c]) for c in range(NP)]
+    stores = [
+        pltpu.make_async_copy(buf.at[c], out.at[:, :, 0, pl.ds(c * W, W)], out_sem.at[c])
+        for c in range(NP)
+    ]
+    for c in loads:
+        c.start()
+    for n in range(NP):
+        loads[n].wait()
+        stores[n].start()
+    for c in stores:
+        c.wait()
+
+
+def in_place(panels):
+    any_spec = pl.BlockSpec(memory_space=pl.ANY)
+    sems = pltpu.SemaphoreType.DMA((NP,))
+    return pl.pallas_call(
+        write_out,
+        out_shape=jax.ShapeDtypeStruct((2, UNK, 1, 512), f32),
+        in_specs=[any_spec],
+        out_specs=any_spec,
+        scratch_shapes=[pltpu.VMEM((NP, 2, UNK, W), f32), sems, sems],
+        compiler_params=pltpu.CompilerParams(vmem_limit_bytes=60 * 1024 * 1024),
+    )(panels)
+
+
 def per_device(right_side, start_field, block_inverse, upwind_block, south_block, north_block):
     def rows_first(a):
         return jnp.transpose(a, (0, 2, 1, 3))
 
     grid = rows_first(start_field).reshape(2, VARS * NODE, NODE, NODE, 1, 512)
     rest = [rows_first(a) for a in (block_inverse, south_block, north_block, upwind_block, right_side)]
-    return rows_first(solve(grid, *rest))
+    return rows_first(in_place(solve(grid, *rest)))
 
 
 def solution(mesh):

time: 69.6 us -> 69.4 us (level)
  the two profiles are of different devices: /device:TPU:2 before, /device:TPU:6 now
where the time goes in v3:
time: 69.4 us; the launch traced here: 69.3 us
  Pallas kernels  69.3 us (100%)
    pallas_call x1, Pallas kernels, solve(): pl.pallas_call(kernel, out_shape=jax.ShapeDtypeStruct((NP, 2, UNK, W), f3...  66.6 us
    pallas_call x1, Pallas kernels, in_place(): pl.pallas_call(write_out, out_shape=jax.ShapeDtypeStruct((2, UNK, 1, 512)...  2.62 us

profile of v3, /device:TPU:6, one launch (start us, length us, event | category | flops | bytes accessed | tf_op | source)
XLA Modules:
  0.0 69.3 jit_solution(9792245195533403709)
XLA Ops:
  0.0 66.6 %shard_map.64.panels = f32[4,2,625,128]{3,2,1,0:T(8,128)} custom-call(f32[2,25,5,5,1,512]{5,4,3,2,1,0:T(1,128)} %bitcast.8, f32[2,625,1,625]{3,2,1,0:T(1,128)} %bitcast.7, f32[2,625,1,125]{3,2,1,0:T(1,128)} %bitcast.10, f32[2,625,1,125]{3,2,1,0:T(1,128)} %bitcast.11, f32[2,625,1,125]{3,2,1,0:T(1,128)} %bitcast.12, f32[2,625,1,512]{3,2,1,0:T(1,128)} %bitcast.9), custom_call_target="tpu_custom_call" | custom-call | tf_op jit(solution)/shard_map/pallas_call | solution.py:467
  66.6 2.6 %shard_map.65 = f32[2,625,1,512]{3,2,1,0:T(1,128)} custom-call(f32[4,2,625,128]{3,2,1,0:T(8,128)} %shard_map.64.panels), custom_call_target="tpu_custom_call" | custom-call | tf_op jit(solution)/shard_map/pallas_call | solution.py:497

commit v4 on v3

--- a/solution.py
+++ b/solution.py
@@ -47,7 +47,7 @@
 def kernel(
     start, b_in, s_in, n_in, u_in, f_in,
     out,
-    bst, sust, fst, sh, sl, fh, fl, dbst, hbst, bch, bcl, bfp, bsn3, bu3, hsn3, hu3, hlf, snr,
+    bst, sust, fst, db5, sh, sl, fh, fl, dbst, hbst, bch, bcl, bfp, bsn3, bu3, hsn3, hu3, hlf, snr,
     gsn3, dsn3, m3, gf, g0f, phi, phik, coef, ca3, e3, phi3,
     sn, xq, gown, gpar, g0c, g0v, ag, xs, xb, tp, tin, ts, zs, hb, ob,
     load_sem, out_sem, zsend, zrecv, gsend, grecv, asend, arecv, xsend, xrecv, tsend, trecv,
@@ -125,7 +125,11 @@
         return remote(phik.at[k], phik.at[k], ksend.at[d - 1], krecv.at[k], {"sweep": ring_peer(d)})
 
     b_load = load(b_in.at[:, :, 0, :], bst, 0)
-    b_load.start()
+    d_loads = [
+        load(b_in.at[:, pl.ds(125 * v + 100, 25), 0, :], db5.at[v], 5 + v) for v in range(VARS)
+    ]
+    for c in d_loads:
+        c.start()
     su_loads = [load(m.at[:, :, 0, :], sust.at[n], 1 + n) for n, m in enumerate((s_in, n_in, u_in))]
     for c in su_loads:
         c.start()
@@ -146,16 +150,17 @@
         for ref in (fh, fl):
             ref[e, U - 16:, :] = jnp.zeros((16, 512), bf16)
 
-    b_load.wait()
-    for e in range(2):
-        for v in range(VARS):
-            dbst[e, 25 * v:25 * v + 25, :UNK] = bst[e, 125 * v + 100:125 * v + 125, :]
+    for v in range(VARS):
+        d_loads[v].wait()
+        for e in range(2):
+            dbst[e, 25 * v:25 * v + 25, :UNK] = db5[v, e]
     for n in range(3):
         su_loads[n].wait()
         for e in range(2):
             hi, lo = halves(sust[n, e])
             sh[e, :UNK, F * n:F * n + FACE] = hi
             sl[e, :UNK, F * n:F * n + FACE] = lo
+    b_load.start()
     dsnu = []
     dbs = []
     for e in range(2):
@@ -191,9 +196,11 @@
     for d in (1, 2, 3):
         kcopy(d).start()
 
-    def blocks(start_at):
-        def one(i, _):
-            n = start_at + i
+    def chunks_by(k):
+        return jnp.clip(k - 5, 0, 2) + 2 * jnp.clip(k - 7, 0, 3)
+
+    def blocks(first, last):
+        def one(n, _):
             e = n // 4
             m = lax.rem(n, 4)
             rows = pl.ds(pl.multiple_of(m * 160, 160), 160)
@@ -220,7 +227,7 @@
                 bfp[c, e, rows, :] = r[:, W * c:W * c + W]
             return 0
 
-        lax.fori_loop(0, 1, one, 0)
+        lax.fori_loop(first, last, one, 0)
 
     def face_rows(e):
         for g in range(25):
@@ -398,13 +405,17 @@
         def _():
             coefficients()
 
+        @pl.when(k == 0)
+        def _():
+            b_load.wait()
+
         @pl.when(k < 2)
         def _():
             face_rows(k)
 
-        @pl.when(jnp.logical_and(k >= 2, k < 10))
-        def _():
-            blocks(k - 2)
+        @pl.when(jnp.logical_and(k >= 5, k < 10))
+        def _():
+            blocks(chunks_by(k), chunks_by(k + 1))
 
 
         return 0
@@ -448,6 +459,7 @@
     D = pltpu.SemaphoreType.DMA
     scratch = [
         V((2, UNK, UNK), f32), V((3, 2, UNK, FACE), f32), V((2, UNK, 512), f32),
+        V((VARS, 2, 25, UNK), f32),
         V((2, U, 3 * F), bf16), V((2, U, 3 * F), bf16), V((2, U, 512), bf16), V((2, U, 512), bf16),
         V((2, F, U), f32), V((2 * F, U), f32), V((160, U), bf16), V((160, U), bf16),
         V((NP, 2, U, W), f32), V((2, U, 6 * F), bf16), V((2, U, 3 * F), bf16),
@@ -460,7 +472,7 @@
         V((NQ, F, W), f32), V((NQ, F, W), f32), V((NQ, RING, F, W), f32), V((NQ, F, W), f32),
         V((NQ, F, W), f32), V((NQ, 2, F, W), f32), V((NQ, F, W), f32), V((NQ, F, W), f32),
         V((NP, 2, 2, F, W), f32), V((NP, 2, 2 * F, W), f32), V((NP, 2, UNK, W), f32),
-        D((5,)), D((NP,)), D((NQ, 2)), D((NQ, 2)), D((NQ,)), D((NQ,)), D((NQ, 3)), D((NQ, RING)),
+        D((10,)), D((NP,)), D((NQ, 2)), D((NQ, 2)), D((NQ,)), D((NQ,)), D((NQ, 3)), D((NQ, RING)),
         D((NQ,)), D((NQ,)), D((NQ,)), D((NQ,)), D, D, D((3,)), D((RING,)),
     ]
     any_spec = pl.BlockSpec(memory_space=pl.ANY)
@@ -477,23 +489,28 @@
 
 
 def write_out(panels, out, buf, load_sem, out_sem):
-    loads = [pltpu.make_async_copy(panels.at[c], buf.at[c], load_sem.at[c]) for c in range(NP)]
+    pieces = [(c, e) for c in range(NP) for e in range(2)]
+    loads = [
+        pltpu.make_async_copy(panels.at[c, e], buf.at[c, e], load_sem.at[c, e]) for c, e in pieces
+    ]
     stores = [
-        pltpu.make_async_copy(buf.at[c], out.at[:, :, 0, pl.ds(c * W, W)], out_sem.at[c])
-        for c in range(NP)
+        pltpu.make_async_copy(
+            buf.at[c, e], out.at[e, :, 0, pl.ds(c * W, W)], out_sem.at[c, e]
+        )
+        for c, e in pieces
     ]
     for c in loads:
         c.start()
-    for n in range(NP):
-        loads[n].wait()
-        stores[n].start()
+    for a, b in zip(loads, stores):
+        a.wait()
+        b.start()
     for c in stores:
         c.wait()
 
 
 def in_place(panels):
     any_spec = pl.BlockSpec(memory_space=pl.ANY)
-    sems = pltpu.SemaphoreType.DMA((NP,))
+    sems = pltpu.SemaphoreType.DMA((NP, 2))
     return pl.pallas_call(
         write_out,
         out_shape=jax.ShapeDtypeStruct((2, UNK, 1, 512), f32),

time: 69.4 us -> 67 us (0.965)
  Pallas kernels: 69.3 us -> 66.8 us
    pallas_call x1, Pallas kernels: 66.6 us -> 64.3 us  [solve(): pl.pallas_call(kernel, out_shape=jax.ShapeDtypeStruct((NP, 2, UNK, W), f3...]
where the time goes in v4:
time: 67 us; the launch traced here: 66.9 us
  Pallas kernels  66.8 us (100%)
    pallas_call x1, Pallas kernels, solve(): pl.pallas_call(kernel, out_shape=jax.ShapeDtypeStruct((NP, 2, UNK, W), f3...  64.3 us
    pallas_call x1, Pallas kernels, in_place(): pl.pallas_call(write_out, out_shape=jax.ShapeDtypeStruct((2, UNK, 1, 512)...  2.57 us

profile of v4, /device:TPU:6, one launch (start us, length us, event | category | flops | bytes accessed | tf_op | source)
XLA Modules:
  0.0 66.9 jit_solution(15092688814925960256)
XLA Ops:
  0.0 64.3 %shard_map.64.panels = f32[4,2,625,128]{3,2,1,0:T(8,128)} custom-call(f32[2,25,5,5,1,512]{5,4,3,2,1,0:T(1,128)} %bitcast.8, f32[2,625,1,625]{3,2,1,0:T(1,128)} %bitcast.7, f32[2,625,1,125]{3,2,1,0:T(1,128)} %bitcast.10, f32[2,625,1,125]{3,2,1,0:T(1,128)} %bitcast.11, f32[2,625,1,125]{3,2,1,0:T(1,128)} %bitcast.12, f32[2,625,1,512]{3,2,1,0:T(1,128)} %bitcast.9), custom_call_target="tpu_custom_call" | custom-call | tf_op jit(solution)/shard_map/pallas_call | solution.py:479
  64.3 2.6 %shard_map.65 = f32[2,625,1,512]{3,2,1,0:T(1,128)} custom-call(f32[4,2,625,128]{3,2,1,0:T(8,128)} %shard_map.64.panels), custom_call_target="tpu_custom_call" | custom-call | tf_op jit(solution)/shard_map/pallas_call | solution.py:514

commit v5 on v4

--- a/solution.py
+++ b/solution.py
@@ -76,53 +76,6 @@
     for dev in ({"span": up}, {"span": down}, {"sweep": mate}, {"sweep": over},
                 {"sweep": ring_peer(1)}, {"sweep": ring_peer(2)}, {"sweep": ring_peer(3)}):
         pl.semaphore_signal(barrier, inc=1, device_id=dev, device_id_type=MESH)
-    pl.semaphore_wait(barrier, 7)
-
-    def remote(src, dst, ss, rs, dev):
-        return pltpu.make_async_remote_copy(
-            src_ref=src, dst_ref=dst, send_sem=ss, recv_sem=rs, device_id=dev, device_id_type=MESH
-        )
-
-    def zdev(way):
-        return {"span": up if way == 0 else down}
-
-    def zcopy1(c, way):
-        level = NODE - 1 if way == 0 else 0
-        src = start.at[:, :, level, :, 0, pl.ds(pl.multiple_of(c * W, W), W)]
-        return remote(src, snr.at[c, way], zsend.at[c, way], zrecv.at[c, way], zdev(way))
-
-    def zcopy2(q, way):
-        c = lax.rem(q, NP)
-        return remote(zs.at[c, way], sn.at[q, way], zsend.at[q, way], zrecv.at[q, way], zdev(way))
-
-    for c in range(NP):
-        for way in range(2):
-            zcopy1(c, way).start()
-    def gcopy(q):
-        return remote(gown.at[q], gpar.at[q], gsend.at[q], grecv.at[q], {"sweep": mate})
-
-    def acopy(q, d):
-        return remote(ag.at[q, y], ag.at[q, y], asend.at[q, d - 1], arecv.at[q, y], {"sweep": ring_peer(d)})
-
-    def aland(q, d):
-        k = lax.rem(y + RING - d, RING)
-        return remote(ag.at[q, k], ag.at[q, k], asend.at[q, d - 1], arecv.at[q, k], {"sweep": ring_peer(d)})
-
-    def xcopy(q):
-        return remote(xs.at[q], xb.at[q], xsend.at[q], xrecv.at[q], {"sweep": over})
-
-    def tcopy(q):
-        return remote(ts.at[q], tin.at[q], tsend.at[q], trecv.at[q], {"sweep": mate})
-
-    def pcopy():
-        return remote(phi.at[core], phi.at[core], psend, precv, {"sweep": mate})
-
-    def kcopy(d):
-        return remote(phik.at[y], phik.at[y], ksend.at[d - 1], krecv.at[y], {"sweep": ring_peer(d)})
-
-    def kland(d):
-        k = lax.rem(y + RING - d, RING)
-        return remote(phik.at[k], phik.at[k], ksend.at[d - 1], krecv.at[k], {"sweep": ring_peer(d)})
 
     b_load = load(b_in.at[:, :, 0, :], bst, 0)
     d_loads = [
@@ -135,6 +88,54 @@
         c.start()
     f_load = load(f_in.at[:, :, 0, :], fst, 4)
     f_load.start()
+
+    pl.semaphore_wait(barrier, 7)
+
+    def remote(src, dst, ss, rs, dev):
+        return pltpu.make_async_remote_copy(
+            src_ref=src, dst_ref=dst, send_sem=ss, recv_sem=rs, device_id=dev, device_id_type=MESH
+        )
+
+    def zdev(way):
+        return {"span": up if way == 0 else down}
+
+    def zcopy1(c, way):
+        level = NODE - 1 if way == 0 else 0
+        src = start.at[:, :, level, :, 0, pl.ds(pl.multiple_of(c * W, W), W)]
+        return remote(src, snr.at[c, way], zsend.at[c, way], zrecv.at[c, way], zdev(way))
+
+    def zcopy2(q, way):
+        c = lax.rem(q, NP)
+        return remote(zs.at[c, way], sn.at[q, way], zsend.at[q, way], zrecv.at[q, way], zdev(way))
+
+    for c in range(NP):
+        for way in range(2):
+            zcopy1(c, way).start()
+    def gcopy(q):
+        return remote(gown.at[q], gpar.at[q], gsend.at[q], grecv.at[q], {"sweep": mate})
+
+    def acopy(q, d):
+        return remote(ag.at[q, y], ag.at[q, y], asend.at[q, d - 1], arecv.at[q, y], {"sweep": ring_peer(d)})
+
+    def aland(q, d):
+        k = lax.rem(y + RING - d, RING)
+        return remote(ag.at[q, k], ag.at[q, k], asend.at[q, d - 1], arecv.at[q, k], {"sweep": ring_peer(d)})
+
+    def xcopy(q):
+        return remote(xs.at[q], xb.at[q], xsend.at[q], xrecv.at[q], {"sweep": over})
+
+    def tcopy(q):
+        return remote(ts.at[q], tin.at[q], tsend.at[q], trecv.at[q], {"sweep": mate})
+
+    def pcopy():
+        return remote(phi.at[core], phi.at[core], psend, precv, {"sweep": mate})
+
+    def kcopy(d):
+        return remote(phik.at[y], phik.at[y], ksend.at[d - 1], krecv.at[y], {"sweep": ring_peer(d)})
+
+    def kland(d):
+        k = lax.rem(y + RING - d, RING)
+        return remote(phik.at[k], phik.at[k], ksend.at[d - 1], krecv.at[k], {"sweep": ring_peer(d)})
 
     edge = pl.ds(U - F, F)
     hbst[:, edge] = jnp.zeros((2 * F, F), f32)

time: 67 us -> 67 us (level)
  no operation moved by 1% of the time
where the time goes in v5:
time: 67 us; the launch traced here: 66.9 us
  Pallas kernels  66.9 us (100%)
    pallas_call x1, Pallas kernels, solve(): pl.pallas_call(kernel, out_shape=jax.ShapeDtypeStruct((NP, 2, UNK, W), f3...  64.3 us
    pallas_call x1, Pallas kernels, in_place(): pl.pallas_call(write_out, out_shape=jax.ShapeDtypeStruct((2, UNK, 1, 512)...  2.57 us

profile of v5, /device:TPU:6, one launch (start us, length us, event | category | flops | bytes accessed | tf_op | source)
XLA Modules:
  0.0 66.9 jit_solution(12659912644029199871)
XLA Ops:
  0.0 64.3 %shard_map.64.panels = f32[4,2,625,128]{3,2,1,0:T(8,128)} custom-call(f32[2,25,5,5,1,512]{5,4,3,2,1,0:T(1,128)} %bitcast.8, f32[2,625,1,625]{3,2,1,0:T(1,128)} %bitcast.7, f32[2,625,1,125]{3,2,1,0:T(1,128)} %bitcast.10, f32[2,625,1,125]{3,2,1,0:T(1,128)} %bitcast.11, f32[2,625,1,125]{3,2,1,0:T(1,128)} %bitcast.12, f32[2,625,1,512]{3,2,1,0:T(1,128)} %bitcast.9), custom_call_target="tpu_custom_call" | custom-call | tf_op jit(solution)/shard_map/pallas_call | solution.py:480
  64.3 2.6 %shard_map.65 = f32[2,625,1,512]{3,2,1,0:T(1,128)} custom-call(f32[4,2,625,128]{3,2,1,0:T(8,128)} %shard_map.64.panels), custom_call_target="tpu_custom_call" | custom-call | tf_op jit(solution)/shard_map/pallas_call | solution.py:515
